TPU v7x, 128 devices: a whole 4x4x4 slice. The times are simulated.
128 devices in a mesh: lat: 16 (over y, z_hi, core), chan: 8 (over z_lo, x).
Axes of the slice: x: 4, y: 4, z: 4 (z_hi: 2, z_lo: 2; z = z_hi * 2 + z_lo), core: 2. Of those that a mesh axis runs over, the one named last changes fastest.
Arguments:
- state: bfloat16 [64, 512, 1024], P('lat', None, 'chan'), may hold values from -15 to 15
- background: bfloat16 [64, 512, 1024], P('lat', None, 'chan'), may hold values from -15.5 to 15.5
- gain: float32 [1024], replicated, may hold values from 0.5 to 2
- w_query: bfloat16 [1024, 1024], P(None, 'chan'), may hold values from -0.2 to 0.2
- w_key: bfloat16 [1024, 1024], P(None, 'chan'), may hold values from -5 to 5
- w_value: bfloat16 [1024, 1024], P(None, 'chan'), may hold values from -0.1875 to 0.1875
- w_out: bfloat16 [1024, 1024], P('chan'), may hold values from -0.75 to 0.75
- decoder: bfloat16 [1024, 69], P('chan'), may hold values from -0.1875 to 0.1875
- interp: bfloat16 [16, 8, 16, 16, 128, 128], P('lat', 'chan'), may hold values from -0.5 to 0.5
- obs_values: bfloat16 [16, 8, 16, 16, 128], P('lat', 'chan'), may hold values from -6 to 6
- tile_index: int32 [16, 8, 16, 16], P('lat', 'chan'), may hold values from 0 to 1103
- block_count: int32 [16, 8, 16], P('lat', 'chan'), may hold values from 1 to 16, as said below
Outputs:
- misfit: float32 [16, 8, 16, 16, 128], P(None, 'chan', 'lat')
- gradient: float32 [64, 512, 1024], P('lat', None, 'chan')
Inputs may be any that keep to these rules, and one draw needn't show every extreme that they name: `tile_index`: A tile index n names variable n // 16 and the run n % 16 of 128 tokens of the target band. Live slots are the first block_count ones; every draw has a target band that receives 16 blocks from every owner and channel group.
All inputs are finite; a program needn't handle non-finite values.
Results may differ from a plain program's by a relative error of at most 0.02.
The roundings to bfloat16 on the way count: a program that leaves them out, or rounds other values in their place, can miss the bound.
Values may be sent and summed in bfloat16 or wider, within the bound.
A program may use at most 128 MiB of HBM per device.

v0:
```python
import jax
import jax.numpy as jnp
from jax import lax
from jax.sharding import PartitionSpec as P

D = 1024
HD = 64
VARS = 69
CELLS = 128
WC = 256
NC = 512
EPSILON = 1e-05
NEGATIVE = -1e30


def with_halo(array, sides, width):
    for axis, dim in sides:
        size, length = (lax.axis_size(axis), array.shape[dim])
        up = [(i, (i + 1) % size) for i in range(size - 1)]
        down = [(j, i) for i, j in up]
        last = lax.slice_in_dim(array, length - width, length, axis=dim)
        initial = lax.slice_in_dim(array, 0, width, axis=dim)
        before = lax.ppermute(last, axis, up)
        after = lax.ppermute(initial, axis, down)
        array = jnp.concatenate([before, array, after], axis=dim)
    return array


def in_blocks(array, dim, length):
    lengths = array.shape
    parts = array.reshape(*lengths[:dim], length, lengths[dim] // length, *lengths[dim + 1 :])
    return jnp.moveaxis(parts, dim, 0)


def sent_and_summed(array, axis, dim):
    length = lax.axis_size(axis)
    parts = lax.all_to_all(in_blocks(array, dim, length), axis, 0, 0, tiled=True)
    return jnp.sum(parts.astype(jnp.float32), axis=0)


def from_everyone(array, axis):
    copies = jnp.broadcast_to(array, (lax.axis_size(axis), *array.shape))
    return lax.all_to_all(copies, axis, split_axis=0, concat_axis=0, tiled=True)


def of_everyone(array, axis):
    everything = from_everyone(array, axis)
    return jnp.sum(everything.astype(jnp.float32), axis=0)


def in_one_piece(arrays, axis, split_dim, concat_dim, along):
    ends, at = ([], 0)
    for a in arrays[:-1]:
        at += a.shape[along]
        ends.append(at)
    both = jnp.concatenate(arrays, axis=along)
    return tuple(
        jnp.split(
            lax.all_to_all(both, axis, split_axis=split_dim, concat_axis=concat_dim, tiled=True),
            ends,
            axis=along,
        )
    )


def taken_together(array, axis):
    everything = from_everyone(array, axis)
    return jnp.sum(everything, axis=0)


def in_one(arrays, axis):
    ends = [0]
    for a in arrays:
        ends.append(ends[-1] + a.size)
    total = taken_together(jnp.concatenate([a.ravel() for a in arrays]), axis)
    return tuple((total[b:e].reshape(a.shape) for a, b, e in zip(arrays, ends, ends[1:])))


def normalize(state_rows):
    average = jnp.mean(state_rows, axis=-1, keepdims=True)
    centred = state_rows - average
    variance = jnp.mean(centred * centred, axis=-1, keepdims=True)
    inverse = lax.rsqrt(variance + EPSILON)
    return (centred * inverse, inverse)


def window_keys(padded, rows_band):
    stacked = jnp.stack(
        [padded[0:rows_band], padded[1 : rows_band + 1], padded[2 : rows_band + 2]], axis=1
    )
    shaped = stacked.reshape(rows_band, 3, NC // WC, WC, stacked.shape[3], stacked.shape[4])
    shaped = jnp.transpose(shaped, (0, 2, 1, 3, 4, 5))
    return shaped.reshape(rows_band, NC // WC, 3 * WC, stacked.shape[3], stacked.shape[4])


def key_mask(valid_rows):
    rows_band = valid_rows.shape[0] - 2
    triple = jnp.stack(
        [valid_rows[0:rows_band], valid_rows[1 : rows_band + 1], valid_rows[2 : rows_band + 2]],
        axis=1,
    )
    spread = jnp.repeat(triple, WC, axis=1)
    return spread[:, None, None, None, :]


def attend_forward(queries, keys_win, values_win, key_valid):
    scores = jnp.einsum(
        "rwihd,rwjhd->rwhij", queries, keys_win, preferred_element_type=jnp.float32
    ) * HD ** (-0.5)
    scores = jnp.where(key_valid, scores, NEGATIVE)
    highest = jnp.max(scores, axis=-1, keepdims=True)
    exponent = jnp.exp(scores - highest)
    attention = exponent / jnp.sum(exponent, axis=-1, keepdims=True)
    attention_low = attention.astype(jnp.bfloat16)
    mixed_heads = jnp.einsum(
        "rwhij,rwjhd->rwihd", attention_low, values_win, preferred_element_type=jnp.float32
    ).astype(jnp.bfloat16)
    return (attention, attention_low, mixed_heads)


def attend_backward(queries, keys_win, values_win, attention, attention_low, grad_mixed):
    grad_probs = jnp.einsum(
        "rwihd,rwjhd->rwhij", grad_mixed, values_win, preferred_element_type=jnp.float32
    )
    row_delta = jnp.sum(attention * grad_probs, axis=-1, keepdims=True)
    grad_scores = (attention * (grad_probs - row_delta) * HD ** (-0.5)).astype(jnp.bfloat16)
    grad_queries = jnp.einsum(
        "rwhij,rwjhd->rwihd", grad_scores, keys_win, preferred_element_type=jnp.float32
    ).astype(jnp.bfloat16)
    grad_keys = jnp.einsum(
        "rwhij,rwihd->rwjhd", grad_scores, queries, preferred_element_type=jnp.float32
    )
    grad_values = jnp.einsum(
        "rwhij,rwihd->rwjhd", attention_low, grad_mixed, preferred_element_type=jnp.float32
    )
    return (grad_queries, grad_keys, grad_values)


def unwindow(windowed, rows_band):
    width_heads = windowed.shape[3] * windowed.shape[4]
    shaped = windowed.reshape(rows_band, NC // WC, 3, WC, width_heads)
    shaped = jnp.transpose(shaped, (0, 2, 1, 3, 4)).reshape(rows_band, 3, NC, width_heads)
    summed = jnp.zeros((rows_band + 2, NC, width_heads), jnp.float32)
    for offset in range(3):
        summed = summed.at[offset : offset + rows_band].add(shaped[:, offset])
    return summed


def contract_last(left_rows, right_rows):
    return lax.dot_general(
        left_rows, right_rows, (((1,), (1,)), ((), ())), preferred_element_type=jnp.float32
    )


def body(
    state,
    background,
    gain,
    w_query,
    w_key,
    w_value,
    w_out,
    decoder,
    interp,
    obs_values,
    tile_index,
    block_count,
):
    rows_band, columns, width_local = state.shape
    tokens = rows_band * columns
    heads_local = width_local // HD
    chan_pos = lax.axis_index("chan")
    lat_pos = lax.axis_index("lat")
    lat_count = lax.axis_size("lat")
    wide_state = lax.all_gather(state, "chan", axis=2, tiled=True)
    hat_rows, inverse = normalize(wide_state.astype(jnp.float32).reshape(tokens, D))
    normed = (hat_rows * gain).astype(jnp.bfloat16)
    queries = jnp.dot(normed, w_query, preferred_element_type=jnp.float32).astype(jnp.bfloat16)
    keys_local = jnp.dot(normed, w_key, preferred_element_type=jnp.float32).astype(jnp.bfloat16)
    values_local = jnp.dot(normed, w_value, preferred_element_type=jnp.float32).astype(jnp.bfloat16)
    key_pair = jnp.stack([keys_local, values_local]).reshape(2, rows_band, columns, width_local)
    padded = with_halo(key_pair, (("lat", 1),), 1)
    global_rows = lat_pos * rows_band + jnp.arange(rows_band + 2, dtype=jnp.int32) - 1
    valid_rows = (global_rows >= 0) & (global_rows < lat_count * rows_band)
    key_valid = key_mask(valid_rows)
    keys_win = window_keys(padded[0].reshape(rows_band + 2, columns, heads_local, HD), rows_band)
    values_win = window_keys(padded[1].reshape(rows_band + 2, columns, heads_local, HD), rows_band)
    query_win = queries.reshape(rows_band, columns // WC, WC, heads_local, HD)
    attention, attention_low, mixed_heads = attend_forward(
        query_win, keys_win, values_win, key_valid
    )
    attn_part = jnp.dot(
        mixed_heads.reshape(tokens, width_local), w_out, preferred_element_type=jnp.float32
    )
    attn_sum = sent_and_summed(
        attn_part.reshape(rows_band, columns, D).astype(jnp.bfloat16), "chan", 2
    )
    updated = (state.astype(jnp.float32) + attn_sum).astype(jnp.bfloat16)
    fields_part = lax.dot_general(
        decoder,
        updated.reshape(tokens, width_local),
        (((0,), (1,)), ((), ())),
        preferred_element_type=jnp.float32,
    )
    fields = of_everyone(fields_part.astype(jnp.bfloat16), "chan").astype(jnp.float32)
    tiles_here = fields.astype(jnp.bfloat16).reshape(VARS * (tokens // CELLS), CELLS)
    slot_ids = jnp.arange(tile_index.shape[-1], dtype=jnp.int32)
    tiles_in = lax.all_to_all(tile_index, "lat", split_axis=2, concat_axis=0, tiled=True)
    sent_tiles = tiles_here[tiles_in]
    picked = lax.all_to_all(sent_tiles, "lat", split_axis=0, concat_axis=2, tiled=True)
    predicted = jnp.einsum(
        "abcsok,abcsk->abcso", interp, picked, preferred_element_type=jnp.float32
    )
    live_slot = slot_ids < block_count[..., None]
    own_misfit = jnp.where(live_slot[..., None], predicted - obs_values.astype(jnp.float32), 0.0)
    own_adjoint = jnp.einsum(
        "abcsok,abcso->abcsk",
        interp,
        own_misfit.astype(jnp.bfloat16),
        preferred_element_type=jnp.float32,
    )
    adjoint, misfit = tuple(
        (
            part.astype(jnp.float32)
            for part in in_one_piece(
                (own_adjoint.astype(jnp.bfloat16), own_misfit.astype(jnp.bfloat16)), "lat", 2, 0, 1
            )
        )
    )
    grad_tiles = (
        jnp.zeros((tiles_here.shape[0], CELLS), jnp.float32)
        .at[tiles_in.reshape(-1)]
        .add(adjoint.reshape(-1, CELLS))
    )
    grad_tiles = of_everyone(grad_tiles.astype(jnp.bfloat16), "chan").astype(jnp.float32)
    grad_field = grad_tiles.reshape(VARS, tokens)
    grad_update = lax.dot_general(
        grad_field,
        decoder.astype(jnp.float32),
        (((0,), (1,)), ((), ())),
        precision=lax.Precision.HIGHEST,
    )
    grad_low = grad_update.astype(jnp.bfloat16).reshape(rows_band, columns, width_local)
    portion = lax.all_gather(grad_low, "chan", axis=2, tiled=True)
    grad_mixed = contract_last(portion.reshape(tokens, portion.shape[2]), w_out)
    grad_mixed = grad_mixed.astype(jnp.bfloat16).reshape(
        rows_band, columns // WC, WC, heads_local, HD
    )
    grad_queries, grad_keys_win, grad_values_win = attend_backward(
        query_win, keys_win, values_win, attention, attention_low, grad_mixed
    )
    grad_pair = jnp.stack(
        [unwindow(grad_keys_win, rows_band), unwindow(grad_values_win, rows_band)]
    )
    rim_rows = jnp.stack([grad_pair[:, 0], grad_pair[:, rows_band + 1]], axis=1)
    arrived = with_halo(rim_rows.astype(jnp.bfloat16), (("lat", 1),), 1).astype(rim_rows.dtype)
    own_rows = grad_pair[:, 1 : rows_band + 1]
    own_rows = own_rows.at[:, 0].add(arrived[:, 0])
    own_rows = own_rows.at[:, rows_band - 1].add(arrived[:, 3])
    grad_keys = own_rows[0].astype(jnp.bfloat16).reshape(tokens, width_local)
    grad_values = own_rows[1].astype(jnp.bfloat16).reshape(tokens, width_local)
    grad_part = contract_last(grad_queries.reshape(tokens, width_local), w_query)
    grad_part = grad_part + contract_last(grad_keys, w_key)
    grad_part = grad_part + contract_last(grad_values, w_value)
    grad_normed = lax.psum_scatter(
        grad_part.astype(jnp.bfloat16), "chan", scatter_dimension=1, tiled=True
    ).astype(jnp.float32)
    gain_local = lax.dynamic_slice_in_dim(gain, chan_pos * width_local, width_local, 0)
    hat_local = lax.dynamic_slice_in_dim(hat_rows, chan_pos * width_local, width_local, 1)
    grad_hat = grad_normed * gain_local
    row_sum, cross_sum = in_one(
        (
            jnp.sum(grad_hat, axis=-1, keepdims=True),
            jnp.sum(grad_hat * hat_local, axis=-1, keepdims=True),
        ),
        "chan",
    )
    grad_norm = (grad_hat - row_sum / D - hat_local * (cross_sum / D)) * inverse
    state_flat = state.astype(jnp.float32).reshape(tokens, width_local)
    gradient = (
        state_flat
        - background.astype(jnp.float32).reshape(tokens, width_local)
        + grad_update
        + grad_norm
    )
    return (misfit, gradient.reshape(rows_band, columns, width_local))


def solution(mesh):
    return jax.shard_map(
        body,
        mesh=mesh,
        in_specs=(
            P("lat", None, "chan"),
            P("lat", None, "chan"),
            P(),
            P(None, "chan"),
            P(None, "chan"),
            P(None, "chan"),
            P("chan", None),
            P("chan", None),
            P("lat", "chan", None, None, None, None),
            P("lat", "chan", None, None, None),
            P("lat", "chan", None, None),
            P("lat", "chan", None),
        ),
        out_specs=(P(None, "chan", "lat", None, None), P("lat", None, "chan")),
        check_vma=False,
    )
```

profile of v0, /device:TPU:0, one launch (start us, length us, event | category | flops | bytes accessed | tf_op | source)
XLA Modules:
  0.0 622.9 jit_solution(2726166261618390722)
XLA Ops:
  8.0 63.6 %all-gather.3.cloned.1.call-done = bf16[4,512,1024]{2,1,0:T(8,128)(2,1)} async-done(((bf16[4,512,128]{2,1,0:T(8,128)(2,1)}), bf16[4,512,1024]{2,1,0:T(8,128)(2,1)}) %all-gather.3.cloned.1.call-update) | async-done | bytes 4194320 | tf_op jit(solution)/shard_map/all_gather | solution.py:175
  71.7 3.0 convert_reduce_fusion.2
  76.6 4.0 fusion.8
  80.5 2.0 copy-done.8
  84.4 3.4 convolution_convert_fusion.3
  90.8 2.0 collective-permute-start
  94.3 4.3 convolution_convert_fusion.1
  98.5 3.2 reshape.585
  101.7 3.5 copy.145
  111.6 3.7 maximum_bitcast_fusion.1
  116.6 2.9 reshape.530
  119.5 3.7 maximum_bitcast_fusion
  124.6 3.1 reshape.528
  127.8 10.2 %fusion.81 = (f32[4,2,2,256]{3,2,1,0:T(2,128)S(1)}, f32[4,2,2,256,768]{4,3,2,1,0:T(8,128)}) fusion(pred[4,768]{1,0:T(4,128)(4,1)S(1)} %bitcast.246, bf16[4,2,256,2,64]{2,4,3,1,0:T(8,128)(2,1)S(1)} %copy-done.15, bf16[4,2,768,2,64]{2,4,3,1,0:T(8,128)(2,1)} %reshape.530), kind=kOutput, calls=%fused_computation.131 | convolution fusion | flops 415236864 | bytes 14699520 | tf_op jit(solution)/shard_map/sub | solution.py:112
  138.0 6.7 %fusion.41 = bf16[4,2,256,2,64]{2,4,3,1,0:T(8,128)(2,1)S(1)} fusion(bf16[4,2,768,2,64]{2,4,3,1,0:T(8,128)(2,1)S(1)} %copy-done.4, f32[4,2,2,256,768]{4,3,2,1,0:T(8,128)} %get-tuple-element.134, f32[4,2,2,256]{3,2,1,0:T(2,128)S(1)} %get-tuple-element.133), kind=kOutput, calls=%fused_computation.56 | convolution fusion | flops 409206784 | bytes 14696448 | tf_op jit(solution)/shard_map/rwhij,rwjhd->rwihd/dot_general | solution.py:115
  148.0 54.5 %all_to_all.60 = bf16[8,4,512,128]{3,2,1,0:T(8,128)(2,1)} all-to-all(bf16[8,4,512,128]{3,2,1,0:T(8,128)(2,1)S(1)} %bitcast.221), channel_id=1, replica_groups=mesh['lat'=16,'chan'=8] {'chan'}, dimensions={0} | all-to-all | bytes 8388608 | tf_op jit(solution)/shard_map/all_to_all | solution.py:37
  202.5 9.4 %all-to-all-start.2 = ((s32[1,1,16,16]{3,1,0,2:T(1,128)}), s32[1,1,16,16]{3,1,0,2:T(1,128)S(1)}, u32[]{:S(2)}, u32[]{:S(2)}) async-start(s32[1,1,16,16]{3,1,0,2:T(1,128)} %bitcast.15), calls=%async_computation.2 | async-start | bytes 16384 | tf_op jit(solution)/shard_map/all_to_all | solution.py:208
  211.9 2.9 convert_reduce_fusion
  216.4 3.0 all-to-all-done.2
  221.1 3.7 all-to-all-start.1
  224.9 29.9 %all-to-all-done.1 = bf16[8,69,2048]{2,1,0:T(8,128)(2,1)S(1)} async-done(((bf16[8,69,2048]{2,1,0:T(8,128)(2,1)}), bf16[8,69,2048]{2,1,0:T(8,128)(2,1)S(1)}, u32[]{:S(2)}, u32[]{:S(2)}) %all-to-all-start.1) | async-done | bytes 2261024 | tf_op jit(solution)/shard_map/all_to_all | solution.py:43
  256.9 4.9 all-to-all-start.3
  263.1 6.4 %all-to-all-done.3 = bf16[16,1,1,16,128]{4,3,2,1,0:T(8,128)(2,1)S(1)} async-done(((bf16[16,1,1,16,128]{4,3,2,1,0:T(8,128)(2,1)}), bf16[16,1,1,16,128]{4,3,2,1,0:T(8,128)(2,1)S(1)}, u32[]{:S(2)}, u32[]{:S(2)}) %all-to-all-start.3) | async-done | bytes 65568 | tf_op jit(solution)/shard_map/all_to_all | solution.py:210
  269.5 7.8 %fusion.6 = f32[16,16,1,128]{3,2,1,0:T(1,128)S(1)} fusion(bf16[1,1,16,16,128,128]{5,4,3,2,1,0:T(8,128)(2,1)} %param.36, bf16[16,16,128,1]{2,1,0,3:T(8,128)(2,1)S(1)} %bitcast.237), kind=kOutput, calls=%fused_computation.12 | convolution fusion | flops 8388608 | bytes 8585216 | tf_op jit(solution)/shard_map/abcsok,abcsk->abcso/dot_general | solution.py:211
  277.4 5.7 fusion.4
  283.8 3.5 all-to-all-start.4
  287.3 7.9 %all-to-all-done.4 = bf16[1,2,16,16,128]{4,3,1,0,2:T(8,128)(2,1)S(1)} async-done(((bf16[1,2,16,16,128]{4,3,1,0,2:T(8,128)(2,1)}), bf16[1,2,16,16,128]{4,3,1,0,2:T(8,128)(2,1)S(1)}, u32[]{:S(2)}, u32[]{:S(2)}) %all-to-all-start.4) | async-done | bytes 131104 | tf_op jit(solution)/shard_map/all_to_all | solution.py:59
  297.8 37.8 %all_to_all.61 = bf16[8,1104,128]{2,1,0:T(8,128)(2,1)S(1)} all-to-all(bf16[8,1104,128]{2,1,0:T(8,128)(2,1)S(1)} %broadcast_in_dim.61), channel_id=1, replica_groups=mesh['lat'=16,'chan'=8] {'chan'}, dimensions={0} | all-to-all | bytes 4521984 | tf_op jit(solution)/shard_map/all_to_all | solution.py:43
  336.0 2.2 fusion.82
  338.3 55.6 %all-gather.5.cloned.1.call-done = bf16[4,512,1024]{2,1,0:T(8,128)(2,1)} async-done(((bf16[4,512,128]{2,1,0:T(8,128)(2,1)}), bf16[4,512,1024]{2,1,0:T(8,128)(2,1)}) %all-gather.5.cloned.1.call-update) | async-done | bytes 4194320 | tf_op jit(solution)/shard_map/all_gather | solution.py:244
  393.9 3.4 convolution_convert_fusion
  397.8 2.0 copy.154
  399.7 6.5 %fusion.30 = f32[4,2,768,2,64]{2,4,3,1,0:T(8,128)S(1)} fusion(bf16[4,2,256,2,64]{2,4,3,1,0:T(8,128)(2,1)} %copy.154, f32[4,2,2,256,768]{4,3,2,1,0:T(8,128)} %get-tuple-element.134, f32[4,2,2,256]{3,2,1,0:T(2,128)S(1)} %get-tuple-element.133), kind=kOutput, calls=%fused_computation.48 | convolution fusion | flops 408944640 | bytes 16269312 | tf_op jit(solution)/shard_map/rwhij,rwihd->rwjhd/dot_general | solution.py:133
  406.3 6.3 %fusion.83 = f32[4,2,2,256,768]{4,3,2,1,0:T(8,128)} fusion(bf16[4,2,256,2,64]{2,4,3,1,0:T(8,128)(2,1)S(1)} %copy-done.10, bf16[4,2,768,2,64]{2,4,3,1,0:T(8,128)(2,1)S(1)} %copy-done.5), kind=kOutput, calls=%fused_computation.133 | convolution fusion | flops 402653184 | bytes 14680064 | tf_op jit(solution)/shard_map/rwihd,rwjhd->rwhij/dot_general | solution.py:122
  412.6 33.2 %fusion.44 = bf16[4,2,256,2,64]{2,4,3,1,0:T(8,128)(2,1)} fusion(bf16[4,2,768,2,64]{2,4,3,1,0:T(8,128)(2,1)} %reshape.530, f32[4,2,2,256,768]{4,3,2,1,0:T(8,128)} %fusion.83, f32[4,2,2,256,768]{4,3,2,1,0:T(8,128)} %get-tuple-element.134, f32[4,2,2,256]{3,2,1,0:T(2,128)S(1)} %get-tuple-element.133), kind=kOutput, calls=%fused_computation.57 | convolution fusion | flops 424940288 | bytes 27279360 | tf_op jit(solution)/shard_map/rwhij,rwjhd->rwihd/dot_general | solution.py:127
  445.8 40.1 %fusion.27 = f32[4,2,768,2,64]{2,4,3,1,0:T(8,128)} fusion(bf16[4,2,256,2,64]{2,4,3,1,0:T(8,128)(2,1)} %copy.145, f32[4,2,2,256,768]{4,3,2,1,0:T(8,128)} %fusion.83, f32[4,2,2,256,768]{4,3,2,1,0:T(8,128)} %get-tuple-element.134, f32[4,2,2,256]{3,2,1,0:T(2,128)S(1)} %get-tuple-element.133), kind=kOutput, calls=%fused_computation.47 | convolution fusion | flops 424678144 | bytes 28852224 | tf_op jit(solution)/shard_map/rwhij,rwihd->rwjhd/dot_general | solution.py:130
  485.9 5.9 reshape.545
  491.8 4.9 copy.177
  496.7 4.9 copy.157
  501.6 3.3 reshape.549
  504.9 3.6 copy.179
  513.2 2.2 reshape.544
  524.6 4.0 collective-permute-done.3
  531.0 3.2 add_convert_fusion
  534.2 6.5 %copy.182 = bf16[2048,1024]{0,1:T(8,128)(2,1)} copy(bf16[2048,1024]{1,0:T(8,128)(2,1)} %add_convert_fusion) | data formatting | bytes 8388608
  541.7 59.0 %reduce-scatter.4.cloned.1.call-done = bf16[128,2048]{1,0:T(8,128)(2,1)} async-done(((bf16[1024,2048]{1,0:T(8,128)(2,1)}), bf16[128,2048]{1,0:T(8,128)(2,1)}) %reduce-scatter.4.cloned.1.call-update) | async-done | bytes 524304
  604.0 9.1 %all_to_all.62 = f32[8,1,4096]{2,1,0:T(1,128)S(1)} all-to-all(f32[8,1,4096]{2,1,0:T(1,128)S(1)} %broadcast_in_dim.62), channel_id=1, replica_groups=mesh['lat'=16,'chan'=8] {'chan'}, dimensions={0} | all-to-all | bytes 262144 | tf_op jit(solution)/shard_map/all_to_all | solution.py:43
  613.2 2.9 fusion.58
  (145 shorter events, 52.7 us)
Async XLA Ops:
  7.2 138.4 %copy-start = (bf16[128,1024]{1,0:T(8,128)(2,1)S(1)}, bf16[128,1024]{1,0:T(8,128)(2,1)}, u32[]{:S(2)}) copy-start(bf16[128,1024]{1,0:T(8,128)(2,1)} %param.34) | copy-start | bytes 786436
  7.2 64.5 %all-gather.3.cloned.1.call-start = ((), (), s32[]{:S(2)}) async-start(), calls=%async_computation.8 | async-start | bytes 4718592 | tf_op jit(solution)/shard_map/all_gather | solution.py:175
  8.0 68.5 %copy-start.26 = (f32[1024]{0:T(1024)S(1)}, f32[1024]{0:T(1024)}, u32[]{:S(2)}) copy-start(f32[1024]{0:T(1024)} %param.30) | copy-start | bytes 12292
  71.7 3.4 copy-start.2
  76.5 4.0 copy-start.22
  76.6 5.9 copy-start.19
  80.5 2.0 copy-start.8
  82.5 1.9 copy-start.17
  87.8 0.9 copy-start.12
  90.8 18.1 %collective-permute-start = (bf16[2,1,512,128]{2,3,1,0:T(8,128)(2,1)}, bf16[2,1,512,128]{2,3,1,0:T(8,128)(2,1)}, u32[]{:S(2)}, u32[]{:S(2)}) collective-permute-start(bf16[2,1,512,128]{2,3,1,0:T(8,128)(2,1)} %get-tuple-element.120), channel_id=1, source_target_pairs={{0,8},{8,16},{16,24},{24,32},{32,40},{40,48},{48,56},{56,64},{64,7... | collective-permute-start | bytes 786440 | tf_op jit(solution)/shard_map/ppermute | solution.py:23
  92.8 16.1 %collective-permute-start.1 = (bf16[2,1,512,128]{2,3,1,0:T(8,128)(2,1)}, bf16[2,1,512,128]{2,3,1,0:T(8,128)(2,1)}, u32[]{:S(2)}, u32[]{:S(2)}) collective-permute-start(bf16[2,1,512,128]{2,3,1,0:T(8,128)(2,1)} %get-tuple-element.121), channel_id=1, source_target_pairs={{8,0},{16,8},{24,16},{32,24},{40,32},{48,40},{56,48},{64,56},{72,6... | collective-permute-start | bytes 786440 | tf_op jit(solution)/shard_map/ppermute | solution.py:24
  115.3 4.3 copy-start.13
  123.2 4.5 copy-start.15
  127.8 10.2 %copy-start.4 = (bf16[4,2,768,2,64]{2,4,3,1,0:T(8,128)(2,1)S(1)}, bf16[4,2,768,2,64]{2,4,3,1,0:T(8,128)(2,1)}, u32[]{:S(2)}) copy-start(bf16[4,2,768,2,64]{2,4,3,1,0:T(8,128)(2,1)} %reshape.528) | copy-start | bytes 4718596
  202.5 12.3 %copy-start.11 = (bf16[4,512,128]{2,1,0:T(8,128)(2,1)S(1)}, bf16[4,512,128]{2,1,0:T(8,128)(2,1)}, u32[]{:S(2)}) copy-start(bf16[4,512,128]{2,1,0:T(8,128)(2,1)} %param.28) | copy-start | bytes 1572868
  202.5 12.3 %copy-start.14 = (bf16[4,512,128]{2,1,0:T(8,128)(2,1)S(1)}, bf16[4,512,128]{2,1,0:T(8,128)(2,1)}, u32[]{:S(2)}) copy-start(bf16[4,512,128]{2,1,0:T(8,128)(2,1)} %param.29) | copy-start | bytes 1572868
  202.5 16.9 %all-to-all-start.2 = ((s32[1,1,16,16]{3,1,0,2:T(1,128)}), s32[1,1,16,16]{3,1,0,2:T(1,128)S(1)}, u32[]{:S(2)}, u32[]{:S(2)}) async-start(s32[1,1,16,16]{3,1,0,2:T(1,128)} %bitcast.15), calls=%async_computation.2 | async-start | bytes 16384 | tf_op jit(solution)/shard_map/all_to_all | solution.py:208
  211.9 4.1 copy-start.24
  221.1 40.7 %copy-start.27 = (s32[1,1,16]{2,1,0:T(1,128)S(1)}, s32[1,1,16]{2,1,0:T(1,128)}, u32[]{:S(2)}) copy-start(s32[1,1,16]{2,1,0:T(1,128)} %param.39) | copy-start | bytes 196
  221.1 33.7 %all-to-all-start.1 = ((bf16[8,69,2048]{2,1,0:T(8,128)(2,1)}), bf16[8,69,2048]{2,1,0:T(8,128)(2,1)S(1)}, u32[]{:S(2)}, u32[]{:S(2)}) async-start(bf16[8,69,2048]{2,1,0:T(8,128)(2,1)} %broadcast_in_dim.58), calls=%async_computation.1 | async-start | bytes 4718592 | tf_op jit(solution)/shard_map/all_to_all | solution.py:43
  256.9 12.6 %all-to-all-start.3 = ((bf16[16,1,1,16,128]{4,3,2,1,0:T(8,128)(2,1)}), bf16[16,1,1,16,128]{4,3,2,1,0:T(8,128)(2,1)S(1)}, u32[]{:S(2)}, u32[]{:S(2)}) async-start(bf16[16,1,1,16,128]{4,3,2,1,0:T(8,128)(2,1)} %bitcast.18), calls=%async_computation.3 | async-start | bytes 131072 | tf_op jit(solution)/shard_map/all_to_all | solution.py:210
  269.5 7.8 %copy-start.25 = (bf16[1,1,16,16,128]{4,3,2,1,0:T(8,128)(2,1)S(1)}, bf16[1,1,16,16,128]{4,3,2,1,0:T(8,128)(2,1)}, u32[]{:S(2)}) copy-start(bf16[1,1,16,16,128]{4,3,2,1,0:T(8,128)(2,1)} %param.37) | copy-start | bytes 196612
  283.8 11.5 %all-to-all-start.4 = ((bf16[1,2,16,16,128]{4,3,1,0,2:T(8,128)(2,1)}), bf16[1,2,16,16,128]{4,3,1,0,2:T(8,128)(2,1)S(1)}, u32[]{:S(2)}, u32[]{:S(2)}) async-start(bf16[1,2,16,16,128]{4,3,1,0,2:T(8,128)(2,1)} %pad_maximum_fusion.12), calls=%async_computation.4 | async-start | bytes 262144 | tf_op jit(solution)/shard_map/all_to_all | solution.py:59
  287.3 106.6 %all-gather.5.cloned.1.call-start = ((), (), s32[]{:S(2)}) async-start(), calls=%async_computation.9 | async-start | bytes 4718592 | tf_op jit(solution)/shard_map/all_gather | solution.py:244
  338.3 262.4 %reduce-scatter.4.cloned.1.call-start = ((), (), s32[]{:S(2)}) async-start(), calls=%async_computation.10 | async-start | bytes 4718592
  399.7 6.5 %copy-start.5 = (bf16[4,2,768,2,64]{2,4,3,1,0:T(8,128)(2,1)S(1)}, bf16[4,2,768,2,64]{2,4,3,1,0:T(8,128)(2,1)}, u32[]{:S(2)}) copy-start(bf16[4,2,768,2,64]{2,4,3,1,0:T(8,128)(2,1)} %reshape.528) | copy-start | bytes 4718596
  399.7 6.6 %copy-start.10 = (bf16[4,2,256,2,64]{2,4,3,1,0:T(8,128)(2,1)S(1)}, bf16[4,2,256,2,64]{2,4,3,1,0:T(8,128)(2,1)}, u32[]{:S(2)}) copy-start(bf16[4,2,256,2,64]{2,4,3,1,0:T(8,128)(2,1)} %copy.154) | copy-start | bytes 1572868
  508.5 1.6 copy-start.3
  510.2 1.7 copy-start.16
  520.2 3.0 copy-start.9
  520.2 3.0 copy-start.21
  520.6 4.1 collective-permute-start.2
  521.9 6.8 %collective-permute-start.3 = (bf16[2,1,512,128]{3,2,1,0:T(8,128)(2,1)S(1)}, bf16[2,1,512,128]{3,2,1,0:T(8,128)(2,1)S(1)}, u32[]{:S(2)}, u32[]{:S(2)}) collective-permute-start(bf16[2,1,512,128]{3,2,1,0:T(8,128)(2,1)S(1)} %get-tuple-element.111), channel_id=1, source_target_pairs={{8,0},{16,8},{24,16},{32,24},{40,32},{48,40},{56,48},{64,56},{72,6... | collective-permute-start | bytes 786440 | tf_op jit(solution)/shard_map/ppermute | solution.py:24
  528.8 1.0 copy-start.18
  529.7 1.3 copy-start.20
  540.8 72.5 %copy-start.6 = (f32[4,512,128]{2,1,0:T(8,128)S(1)}, f32[4,512,128]{2,1,0:T(8,128)}, u32[]{:S(2)}) copy-start(f32[4,512,128]{2,1,0:T(8,128)} %get-tuple-element.122) | copy-start | bytes 3145732
  540.8 72.5 %copy-start.7 = (f32[2048,128]{1,0:T(8,128)S(1)}, f32[2048,128]{1,0:T(8,128)}, u32[]{:S(2)}) copy-start(f32[2048,128]{1,0:T(8,128)} %get-tuple-element.136) | copy-start | bytes 3145732
  540.8 72.5 %copy-start.23 = (f32[1,4,4,128]{3,1,2,0:T(4,128)S(1)}, f32[1,4,4,128]{3,1,2,0:T(4,128)}, u32[]{:S(2)}) copy-start(f32[1,4,4,128]{3,1,2,0:T(4,128)} %copy-done.22) | copy-start | bytes 24580
  540.8 75.3 %copy-start.1 = (bf16[128,1024]{1,0:T(8,128)(2,1)S(1)}, bf16[128,1024]{1,0:T(8,128)(2,1)}, u32[]{:S(2)}) copy-start(bf16[128,1024]{1,0:T(8,128)(2,1)} %param.34) | copy-start | bytes 786436
Sparse Core Ops, SparseCore 0:
  9.6 62.0 all-gather.2
  338.4 55.4 all-gather.4
  540.9 59.7 reduce-scatter.3
where the time goes:
time: 629 us; the launch traced here: 623 us
  waiting for transfers between devices  230 us (37%)
  matrix products  139 us (22%)
  blocking collectives  101 us (16%)
  local copies, waits for them, and re-layouts  73.5 us (12%)
  other arithmetic  36.7 us (6%)
  starting transfers between devices  27.7 us (4%)
  between operations  14.7 us (2%)
    all_gather x1, waiting for transfers between devices, body(): wide_state = lax.all_gather(state, 'chan', axis=2, tiled=True)  63.6 us
    unnamed x4, waiting for transfers between devices  59.7 us
    all_gather x1, waiting for transfers between devices, body(): portion = lax.all_gather(grad_low, 'chan', axis=2, tiled=True)  55.6 us
    all_to_all x1, blocking collectives, sent_and_summed(): lax.all_to_all(in_blocks(array, dim, length), axis, 0, 0, tiled=True)  54.5 us
    all_to_all x2, blocking collectives, from_everyone(): return lax.all_to_all(copies, axis, split_axis=0, concat_axis=0, tiled=True)  47 us
    dot_general x1, matrix products, attend_backward(): jnp.einsum('rwhij,rwihd->rwjhd', grad_scores, queries, preferred_element_...  40.1 us
    dot_general x1, matrix products, attend_backward(): jnp.einsum('rwhij,rwjhd->rwihd', grad_scores, keys_win, preferred_element...  33.2 us
    all_to_all x1, waiting for transfers between devices, from_everyone(): return lax.all_to_all(copies, axis, split_axis=0, concat_axis=0, tiled=True)  29.9 us
  transfers between devices with their start and end apart: 11, of which 8 were waited for; matrix products, arithmetic and copies ran while one was open for 4% of the time, Pallas kernels for 0%

commit v1 on v0

--- a/solution.py
+++ b/solution.py
@@ -172,7 +172,9 @@
     chan_pos = lax.axis_index("chan")
     lat_pos = lax.axis_index("lat")
     lat_count = lax.axis_size("lat")
-    wide_state = lax.all_gather(state, "chan", axis=2, tiled=True)
+    wide_state = jnp.concatenate(
+        lax.all_to_all(jnp.stack([state] * lax.axis_size("chan")), "chan", 0, 0), axis=2
+    )
     hat_rows, inverse = normalize(wide_state.astype(jnp.float32).reshape(tokens, D))
     normed = (hat_rows * gain).astype(jnp.bfloat16)
     queries = jnp.dot(normed, w_query, preferred_element_type=jnp.float32).astype(jnp.bfloat16)

time: 629 us -> 651 us (1.035)
  waiting for transfers between devices: 230 us -> 215 us
  blocking collectives: 101 us -> 113 us
  local copies, waits for them, and re-layouts: 73.5 us -> 82.4 us
    all_gather x1 -> x0, waiting for transfers between devices: 63.6 us -> none  [body(): wide_state = lax.all_gather(state, 'chan', axis=2, tiled=True)]
    all_to_all x0 -> x1, waiting for transfers between devices: none -> 49.4 us  [body(): lax.all_to_all(jnp.stack([state] * lax.axis_size('chan')), 'chan', 0, 0)]
    all_to_all x1, blocking collectives: 54.5 us -> 66.1 us  [sent_and_summed(): lax.all_to_all(in_blocks(array, dim, length), axis, 0, 0, tiled=True)]
    convert_element_type x0 -> x2, other arithmetic: none -> 7.33 us  [the longest x1 4.17 us: body(): normed = (hat_rows * gain).astype(jnp.bfloat16)]
    unnamed x4 -> x3, waiting for transfers between devices: 59.7 us -> 59 us
    unnamed x62 -> x60, local copies, waits for them, and re-layouts: 13.3 us -> 12.8 us
where the time goes in v1:
time: 651 us; the launch traced here: 640 us
  waiting for transfers between devices  215 us (33%)
  matrix products  138 us (21%)
  blocking collectives  113 us (17%)
  local copies, waits for them, and re-layouts  82.4 us (13%)
  other arithmetic  41.7 us (6%)
  starting transfers between devices  34 us (5%)
  between operations  15.3 us (2%)
    all_to_all x1, blocking collectives, sent_and_summed(): lax.all_to_all(in_blocks(array, dim, length), axis, 0, 0, tiled=True)  66.1 us
    unnamed x3, waiting for transfers between devices  59 us
    all_gather x1, waiting for transfers between devices, body(): portion = lax.all_gather(grad_low, 'chan', axis=2, tiled=True)  55.6 us
    all_to_all x1, waiting for transfers between devices, body(): lax.all_to_all(jnp.stack([state] * lax.axis_size('chan')), 'chan', 0, 0)  49.4 us
    all_to_all x2, blocking collectives, from_everyone(): return lax.all_to_all(copies, axis, split_axis=0, concat_axis=0, tiled=True)  46.9 us
    dot_general x1, matrix products, attend_backward(): jnp.einsum('rwhij,rwihd->rwjhd', grad_scores, queries, preferred_element_...  40.2 us
    dot_general x1, matrix products, attend_backward(): jnp.einsum('rwhij,rwjhd->rwihd', grad_scores, keys_win, preferred_element...  32.9 us
    all_to_all x1, waiting for transfers between devices, from_everyone(): return lax.all_to_all(copies, axis, split_axis=0, concat_axis=0, tiled=True)  29.9 us
  transfers between devices with their start and end apart: 11, of which 8 were waited for; matrix products, arithmetic and copies ran while one was open for 4% of the time, Pallas kernels for 0%

profile of v1, /device:TPU:0, one launch (start us, length us, event | category | flops | bytes accessed | tf_op | source)
XLA Modules:
  0.0 639.9 jit_solution(1357922281002577611)
XLA Ops:
  7.2 4.1 stack.71
  11.2 5.8 all-to-all-start
  17.1 49.4 %all-to-all-done = bf16[8,4,512,128]{3,2,1,0:T(8,128)(2,1)} async-done(((bf16[8,4,512,128]{3,2,1,0:T(8,128)(2,1)}), bf16[8,4,512,128]{3,2,1,0:T(8,128)(2,1)}, u32[]{:S(2)}, u32[]{:S(2)}) %all-to-all-start) | async-done | bytes 4194336 | tf_op jit(solution)/shard_map/all_to_all | solution.py:176
  66.5 2.8 fusion.20
  69.4 3.0 multiply_reduce_fusion.1
  72.4 3.2 convert_bitcast_fusion
  75.6 4.9 copy.139
  80.5 4.2 multiply_convert_fusion.1
  88.6 3.4 convolution_convert_fusion.3
  98.8 4.3 convolution_convert_fusion.1
  103.1 3.2 reshape.590
  106.3 3.5 copy.149
  116.1 3.7 maximum_bitcast_fusion.1
  121.2 2.9 reshape.534
  124.1 3.7 maximum_bitcast_fusion
  129.2 3.3 reshape.532
  132.6 10.2 %fusion.83 = (f32[4,2,2,256]{3,2,1,0:T(2,128)S(1)}, f32[4,2,2,256,768]{4,3,2,1,0:T(8,128)}) fusion(pred[4,768]{1,0:T(4,128)(4,1)S(1)} %bitcast.254, bf16[4,2,256,2,64]{2,4,3,1,0:T(8,128)(2,1)S(1)} %copy-done.14, bf16[4,2,768,2,64]{2,4,3,1,0:T(8,128)(2,1)} %reshape.534), kind=kOutput, calls=%fused_computation.132 | convolution fusion | flops 415236864 | bytes 14699520 | tf_op jit(solution)/shard_map/sub | solution.py:112
  142.8 6.7 %fusion.42 = bf16[4,2,256,2,64]{2,4,3,1,0:T(8,128)(2,1)S(1)} fusion(bf16[4,2,768,2,64]{2,4,3,1,0:T(8,128)(2,1)S(1)} %copy-done.3, f32[4,2,2,256,768]{4,3,2,1,0:T(8,128)} %get-tuple-element.134, f32[4,2,2,256]{3,2,1,0:T(2,128)S(1)} %get-tuple-element.133), kind=kOutput, calls=%fused_computation.57 | convolution fusion | flops 409206784 | bytes 14696448 | tf_op jit(solution)/shard_map/rwhij,rwjhd->rwihd/dot_general | solution.py:115
  152.8 66.1 %all_to_all.65 = bf16[8,4,512,128]{3,2,1,0:T(8,128)(2,1)} all-to-all(bf16[8,4,512,128]{3,2,1,0:T(8,128)(2,1)S(1)} %bitcast.229), channel_id=1, replica_groups=mesh['lat'=16,'chan'=8] {'chan'}, dimensions={0} | all-to-all | bytes 8388608 | tf_op jit(solution)/shard_map/all_to_all | solution.py:37
  218.9 9.8 %all-to-all-start.3 = ((s32[1,1,16,16]{3,1,0,2:T(1,128)}), s32[1,1,16,16]{3,1,0,2:T(1,128)S(1)}, u32[]{:S(2)}, u32[]{:S(2)}) async-start(s32[1,1,16,16]{3,1,0,2:T(1,128)} %bitcast.15), calls=%async_computation.3 | async-start | bytes 16384 | tf_op jit(solution)/shard_map/all_to_all | solution.py:210
  228.8 2.9 convert_reduce_fusion
  233.3 3.0 all-to-all-done.3
  237.9 3.7 all-to-all-start.2
  241.8 29.9 %all-to-all-done.2 = bf16[8,69,2048]{2,1,0:T(8,128)(2,1)S(1)} async-done(((bf16[8,69,2048]{2,1,0:T(8,128)(2,1)}), bf16[8,69,2048]{2,1,0:T(8,128)(2,1)S(1)}, u32[]{:S(2)}, u32[]{:S(2)}) %all-to-all-start.2) | async-done | bytes 2261024 | tf_op jit(solution)/shard_map/all_to_all | solution.py:43
  273.7 4.7 all-to-all-start.4
  279.9 6.2 all-to-all-done.4
  286.1 7.8 %fusion.7 = f32[16,16,1,128]{3,2,1,0:T(1,128)S(1)} fusion(bf16[1,1,16,16,128,128]{5,4,3,2,1,0:T(8,128)(2,1)} %param.36, bf16[16,16,128,1]{2,1,0,3:T(8,128)(2,1)S(1)} %bitcast.245), kind=kOutput, calls=%fused_computation.14 | convolution fusion | flops 8388608 | bytes 8585216 | tf_op jit(solution)/shard_map/abcsok,abcsk->abcso/dot_general | solution.py:213
  294.0 5.7 fusion.5
  300.4 3.5 all-to-all-start.5
  304.0 7.9 %all-to-all-done.5 = bf16[1,2,16,16,128]{4,3,1,0,2:T(8,128)(2,1)S(1)} async-done(((bf16[1,2,16,16,128]{4,3,1,0,2:T(8,128)(2,1)}), bf16[1,2,16,16,128]{4,3,1,0,2:T(8,128)(2,1)S(1)}, u32[]{:S(2)}, u32[]{:S(2)}) %all-to-all-start.5) | async-done | bytes 131104 | tf_op jit(solution)/shard_map/all_to_all | solution.py:59
  314.4 37.8 %all_to_all.66 = bf16[8,1104,128]{2,1,0:T(8,128)(2,1)S(1)} all-to-all(bf16[8,1104,128]{2,1,0:T(8,128)(2,1)S(1)} %broadcast_in_dim.61), channel_id=1, replica_groups=mesh['lat'=16,'chan'=8] {'chan'}, dimensions={0} | all-to-all | bytes 4521984 | tf_op jit(solution)/shard_map/all_to_all | solution.py:43
  354.9 55.6 %all-gather.2.cloned.1.call-done = bf16[4,512,1024]{2,1,0:T(8,128)(2,1)} async-done(((bf16[4,512,128]{2,1,0:T(8,128)(2,1)}), bf16[4,512,1024]{2,1,0:T(8,128)(2,1)}) %all-gather.2.cloned.1.call-update) | async-done | bytes 4194320 | tf_op jit(solution)/shard_map/all_gather | solution.py:246
  410.5 3.4 convolution_convert_fusion
  416.3 6.5 %fusion.31 = f32[4,2,768,2,64]{2,4,3,1,0:T(8,128)S(1)} fusion(bf16[4,2,256,2,64]{2,4,3,1,0:T(8,128)(2,1)} %copy.158, f32[4,2,2,256,768]{4,3,2,1,0:T(8,128)} %get-tuple-element.134, f32[4,2,2,256]{3,2,1,0:T(2,128)S(1)} %get-tuple-element.133), kind=kOutput, calls=%fused_computation.49 | convolution fusion | flops 408944640 | bytes 16269312 | tf_op jit(solution)/shard_map/rwhij,rwihd->rwjhd/dot_general | solution.py:133
  422.9 6.3 fusion.85
  429.2 32.9 %fusion.45 = bf16[4,2,256,2,64]{2,4,3,1,0:T(8,128)(2,1)} fusion(bf16[4,2,768,2,64]{2,4,3,1,0:T(8,128)(2,1)} %reshape.534, f32[4,2,2,256,768]{4,3,2,1,0:T(8,128)} %fusion.85, f32[4,2,2,256,768]{4,3,2,1,0:T(8,128)} %get-tuple-element.134, f32[4,2,2,256]{3,2,1,0:T(2,128)S(1)} %get-tuple-element.133), kind=kOutput, calls=%fused_computation.58 | convolution fusion | flops 424940288 | bytes 27279360 | tf_op jit(solution)/shard_map/rwhij,rwjhd->rwihd/dot_general | solution.py:127
  462.1 40.2 %fusion.28 = f32[4,2,768,2,64]{2,4,3,1,0:T(8,128)} fusion(bf16[4,2,256,2,64]{2,4,3,1,0:T(8,128)(2,1)} %copy.149, f32[4,2,2,256,768]{4,3,2,1,0:T(8,128)} %fusion.85, f32[4,2,2,256,768]{4,3,2,1,0:T(8,128)} %get-tuple-element.134, f32[4,2,2,256]{3,2,1,0:T(2,128)S(1)} %get-tuple-element.133), kind=kOutput, calls=%fused_computation.48 | convolution fusion | flops 424678144 | bytes 28852224 | tf_op jit(solution)/shard_map/rwhij,rwihd->rwjhd/dot_general | solution.py:130
  502.3 5.9 reshape.549
  508.3 4.9 copy.181
  513.2 4.9 copy.161
  518.0 3.3 reshape.553
  521.3 3.6 copy.183
  541.1 4.0 collective-permute-done.3
  547.5 3.2 add_convert_fusion
  550.7 6.6 %copy.186 = bf16[2048,1024]{0,1:T(8,128)(2,1)} copy(bf16[2048,1024]{1,0:T(8,128)(2,1)} %add_convert_fusion) | data formatting | bytes 8388608
  558.2 59.0 %reduce-scatter.4.cloned.1.call-done = bf16[128,2048]{1,0:T(8,128)(2,1)} async-done(((bf16[1024,2048]{1,0:T(8,128)(2,1)}), bf16[128,2048]{1,0:T(8,128)(2,1)}) %reduce-scatter.4.cloned.1.call-update) | async-done | bytes 524304
  620.4 9.1 %all_to_all.67 = f32[8,1,4096]{2,1,0:T(1,128)S(1)} all-to-all(f32[8,1,4096]{2,1,0:T(1,128)S(1)} %broadcast_in_dim.62), channel_id=1, replica_groups=mesh['lat'=16,'chan'=8] {'chan'}, dimensions={0} | all-to-all | bytes 262144 | tf_op jit(solution)/shard_map/all_to_all | solution.py:43
  629.7 2.9 fusion.59
  (145 shorter events, 61.2 us)
Async XLA Ops:
  7.2 143.2 %copy-start = (bf16[128,1024]{1,0:T(8,128)(2,1)S(1)}, bf16[128,1024]{1,0:T(8,128)(2,1)}, u32[]{:S(2)}) copy-start(bf16[128,1024]{1,0:T(8,128)(2,1)} %param.34) | copy-start | bytes 786436
  11.2 55.3 %all-to-all-start = ((bf16[8,4,512,128]{3,2,1,0:T(8,128)(2,1)}), bf16[8,4,512,128]{3,2,1,0:T(8,128)(2,1)}, u32[]{:S(2)}, u32[]{:S(2)}) async-start(bf16[8,4,512,128]{3,2,1,0:T(8,128)(2,1)} %stack.71), calls=%async_computation | async-start | bytes 8388608 | tf_op jit(solution)/shard_map/all_to_all | solution.py:176
  72.4 8.1 %copy-start.21 = (f32[1,4,4,128]{3,1,2,0:T(4,128)}, f32[1,4,4,128]{3,1,2,0:T(4,128)S(1)}, u32[]{:S(2)}) copy-start(f32[1,4,4,128]{3,1,2,0:T(4,128)S(1)} %copy.199) | copy-start | bytes 24580
  75.6 4.9 copy-start.25
  80.5 6.2 copy-start.18
  84.7 2.0 copy-start.5
  86.6 1.9 copy-start.16
  92.0 0.9 copy-start.11
  95.0 18.5 %collective-permute-start = (bf16[2,1,512,128]{2,3,1,0:T(8,128)(2,1)}, bf16[2,1,512,128]{2,3,1,0:T(8,128)(2,1)}, u32[]{:S(2)}, u32[]{:S(2)}) collective-permute-start(bf16[2,1,512,128]{2,3,1,0:T(8,128)(2,1)} %get-tuple-element.120), channel_id=1, source_target_pairs={{0,8},{8,16},{16,24},{24,32},{32,40},{40,48},{48,56},{56,64},{64,7... | collective-permute-start | bytes 786440 | tf_op jit(solution)/shard_map/ppermute | solution.py:23
  97.3 16.1 %collective-permute-start.1 = (bf16[2,1,512,128]{2,3,1,0:T(8,128)(2,1)}, bf16[2,1,512,128]{2,3,1,0:T(8,128)(2,1)}, u32[]{:S(2)}, u32[]{:S(2)}) collective-permute-start(bf16[2,1,512,128]{2,3,1,0:T(8,128)(2,1)} %get-tuple-element.121), channel_id=1, source_target_pairs={{8,0},{16,8},{24,16},{32,24},{40,32},{48,40},{56,48},{64,56},{72,6... | collective-permute-start | bytes 786440 | tf_op jit(solution)/shard_map/ppermute | solution.py:24
  119.8 4.3 copy-start.12
  127.8 4.7 copy-start.14
  132.6 10.2 %copy-start.3 = (bf16[4,2,768,2,64]{2,4,3,1,0:T(8,128)(2,1)S(1)}, bf16[4,2,768,2,64]{2,4,3,1,0:T(8,128)(2,1)}, u32[]{:S(2)}) copy-start(bf16[4,2,768,2,64]{2,4,3,1,0:T(8,128)(2,1)} %reshape.532) | copy-start | bytes 4718596
  218.9 12.7 %copy-start.9 = (bf16[4,512,128]{2,1,0:T(8,128)(2,1)S(1)}, bf16[4,512,128]{2,1,0:T(8,128)(2,1)}, u32[]{:S(2)}) copy-start(bf16[4,512,128]{2,1,0:T(8,128)(2,1)} %param.28) | copy-start | bytes 1572868
  218.9 12.7 %copy-start.13 = (bf16[4,512,128]{2,1,0:T(8,128)(2,1)S(1)}, bf16[4,512,128]{2,1,0:T(8,128)(2,1)}, u32[]{:S(2)}) copy-start(bf16[4,512,128]{2,1,0:T(8,128)(2,1)} %param.29) | copy-start | bytes 1572868
  218.9 17.3 %all-to-all-start.3 = ((s32[1,1,16,16]{3,1,0,2:T(1,128)}), s32[1,1,16,16]{3,1,0,2:T(1,128)S(1)}, u32[]{:S(2)}, u32[]{:S(2)}) async-start(s32[1,1,16,16]{3,1,0,2:T(1,128)} %bitcast.15), calls=%async_computation.3 | async-start | bytes 16384 | tf_op jit(solution)/shard_map/all_to_all | solution.py:210
  228.8 4.1 copy-start.23
  237.9 40.5 %copy-start.26 = (s32[1,1,16]{2,1,0:T(1,128)S(1)}, s32[1,1,16]{2,1,0:T(1,128)}, u32[]{:S(2)}) copy-start(s32[1,1,16]{2,1,0:T(1,128)} %param.39) | copy-start | bytes 196
  237.9 33.7 %all-to-all-start.2 = ((bf16[8,69,2048]{2,1,0:T(8,128)(2,1)}), bf16[8,69,2048]{2,1,0:T(8,128)(2,1)S(1)}, u32[]{:S(2)}, u32[]{:S(2)}) async-start(bf16[8,69,2048]{2,1,0:T(8,128)(2,1)} %broadcast_in_dim.58), calls=%async_computation.2 | async-start | bytes 4718592 | tf_op jit(solution)/shard_map/all_to_all | solution.py:43
  273.7 12.3 %all-to-all-start.4 = ((bf16[16,1,1,16,128]{4,3,2,1,0:T(8,128)(2,1)}), bf16[16,1,1,16,128]{4,3,2,1,0:T(8,128)(2,1)S(1)}, u32[]{:S(2)}, u32[]{:S(2)}) async-start(bf16[16,1,1,16,128]{4,3,2,1,0:T(8,128)(2,1)} %bitcast.18), calls=%async_computation.4 | async-start | bytes 131072 | tf_op jit(solution)/shard_map/all_to_all | solution.py:212
  286.1 7.8 %copy-start.24 = (bf16[1,1,16,16,128]{4,3,2,1,0:T(8,128)(2,1)S(1)}, bf16[1,1,16,16,128]{4,3,2,1,0:T(8,128)(2,1)}, u32[]{:S(2)}) copy-start(bf16[1,1,16,16,128]{4,3,2,1,0:T(8,128)(2,1)} %param.37) | copy-start | bytes 196612
  300.4 11.5 %all-to-all-start.5 = ((bf16[1,2,16,16,128]{4,3,1,0,2:T(8,128)(2,1)}), bf16[1,2,16,16,128]{4,3,1,0,2:T(8,128)(2,1)S(1)}, u32[]{:S(2)}, u32[]{:S(2)}) async-start(bf16[1,2,16,16,128]{4,3,1,0,2:T(8,128)(2,1)} %pad_maximum_fusion.12), calls=%async_computation.5 | async-start | bytes 262144 | tf_op jit(solution)/shard_map/all_to_all | solution.py:59
  303.9 106.6 %all-gather.2.cloned.1.call-start = ((), (), s32[]{:S(2)}) async-start(), calls=%async_computation.9 | async-start | bytes 4718592 | tf_op jit(solution)/shard_map/all_gather | solution.py:246
  354.9 262.3 %reduce-scatter.4.cloned.1.call-start = ((), (), s32[]{:S(2)}) async-start(), calls=%async_computation.10 | async-start | bytes 4718592
  416.3 6.5 %copy-start.4 = (bf16[4,2,768,2,64]{2,4,3,1,0:T(8,128)(2,1)S(1)}, bf16[4,2,768,2,64]{2,4,3,1,0:T(8,128)(2,1)}, u32[]{:S(2)}) copy-start(bf16[4,2,768,2,64]{2,4,3,1,0:T(8,128)(2,1)} %reshape.532) | copy-start | bytes 4718596
  416.3 6.6 %copy-start.10 = (bf16[4,2,256,2,64]{2,4,3,1,0:T(8,128)(2,1)S(1)}, bf16[4,2,256,2,64]{2,4,3,1,0:T(8,128)(2,1)}, u32[]{:S(2)}) copy-start(bf16[4,2,256,2,64]{2,4,3,1,0:T(8,128)(2,1)} %copy.158) | copy-start | bytes 1572868
  524.9 1.7 copy-start.2
  526.7 1.7 copy-start.15
  536.7 3.0 copy-start.8
  536.7 3.0 copy-start.20
  537.1 4.1 collective-permute-start.2
  538.4 6.8 %collective-permute-start.3 = (bf16[2,1,512,128]{3,2,1,0:T(8,128)(2,1)S(1)}, bf16[2,1,512,128]{3,2,1,0:T(8,128)(2,1)S(1)}, u32[]{:S(2)}, u32[]{:S(2)}) collective-permute-start(bf16[2,1,512,128]{3,2,1,0:T(8,128)(2,1)S(1)} %get-tuple-element.111), channel_id=1, source_target_pairs={{8,0},{16,8},{24,16},{32,24},{40,32},{48,40},{56,48},{64,56},{72,6... | collective-permute-start | bytes 786440 | tf_op jit(solution)/shard_map/ppermute | solution.py:24
  545.2 1.0 copy-start.17
  546.2 1.3 copy-start.19
  557.2 72.4 %copy-start.6 = (f32[4,512,128]{2,1,0:T(8,128)S(1)}, f32[4,512,128]{2,1,0:T(8,128)}, u32[]{:S(2)}) copy-start(f32[4,512,128]{2,1,0:T(8,128)} %get-tuple-element.122) | copy-start | bytes 3145732
  557.2 72.5 %copy-start.7 = (f32[2048,128]{1,0:T(8,128)S(1)}, f32[2048,128]{1,0:T(8,128)}, u32[]{:S(2)}) copy-start(f32[2048,128]{1,0:T(8,128)} %get-tuple-element.136) | copy-start | bytes 3145732
  557.3 72.5 %copy-start.22 = (f32[1,4,4,128]{3,1,2,0:T(4,128)S(1)}, f32[1,4,4,128]{3,1,2,0:T(4,128)}, u32[]{:S(2)}) copy-start(f32[1,4,4,128]{3,1,2,0:T(4,128)} %copy-done.21) | copy-start | bytes 24580
  557.3 75.3 %copy-start.1 = (bf16[128,1024]{1,0:T(8,128)(2,1)S(1)}, bf16[128,1024]{1,0:T(8,128)(2,1)}, u32[]{:S(2)}) copy-start(bf16[128,1024]{1,0:T(8,128)(2,1)} %param.34) | copy-start | bytes 786436
Sparse Core Ops, SparseCore 0:
  355.0 55.4 all-gather.1
  557.4 59.7 reduce-scatter.3
